TPU v7x, 32 devices: a whole 2x2x4 slice. The times are simulated.
32 devices in a mesh: sec: 2 (over x), lat: 16 (over z, y, core).
Axes of the slice: x: 2, y: 2, z: 4, core: 2. Of those that a mesh axis runs over, the one named last changes fastest.
Arguments:
- resid_in: bfloat16 [4, 128, 2048], P('sec', None, 'lat'), may hold values from -6 to 6
- mlp_out: bfloat16 [4, 128, 2048], P('sec', None, 'lat'), may hold values from -6 to 6
- enc_weight: bfloat16 [4, 2048, 1024], P('sec', None, 'lat'), may hold values from -0.125 to 0.125
- enc_bias: float32 [4, 1024], P('sec', 'lat'), may hold values from -3 to 3
- thresholds: int32 [4, 1024], P('sec', 'lat'), may hold values from 0 to 3
- same_dec: bfloat16 [4, 1024, 2048], P('sec', 'lat'), may hold values from -0.1875 to 0.1875
- next_dec: bfloat16 [2, 1024, 2048], P('sec', 'lat'), may hold values from -0.1875 to 0.1875
- cross_dec: bfloat16 [2, 2, 1024, 2048], P('sec', None, 'lat'), may hold values from -0.1875 to 0.1875
Outputs:
- mean_square: float32 [], replicated
- grad_enc: bfloat16 [4, 2048, 1024], P('sec', None, 'lat')
- grad_bias: float32 [4, 1024], P('sec', 'lat')
- grad_same: bfloat16 [4, 1024, 2048], P('sec', 'lat')
- grad_next: bfloat16 [2, 1024, 2048], P('sec', 'lat')
- grad_cross: bfloat16 [2, 2, 1024, 2048], P('sec', None, 'lat')
All inputs are finite; a program needn't handle non-finite values.
Results may differ from a plain program's by a relative error of at most 0.0059.
Values may be sent and summed in bfloat16 or wider, within the bound.
No kernel may reach another device: no remote copies, remote signals or barrier semaphores. Data moves between devices by JAX's collectives and lax.ppermute only.
A program may use at most 64 MiB of HBM per device.

v0:
```python
import jax
import jax.numpy as jnp
from jax import lax
from jax.sharding import PartitionSpec as P

D = 2048
TOKENS = 128
jump_width = 0.1


def shifted(value, axis, steps):
    count = lax.axis_size(axis)
    first, last = (max(0, -steps), min(count, count - steps))
    return lax.ppermute(value, axis, [(source, source + steps) for source in range(first, last)])


def back_dot(grad, weights):
    return lax.dot_general(
        grad, weights, (((1,), (1,)), ((), ())), preferred_element_type=jnp.float32
    )


def outer_dot(act, grad):
    return lax.dot_general(act, grad, (((0,), (0,)), ((), ())), preferred_element_type=jnp.float32)


def per_device(resid_in, mlp_out, enc_weight, enc_bias, thresholds, same_dec, next_dec, cross_dec):
    leading = lax.axis_index("sec") == 0
    inputs_full = lax.all_gather(resid_in, "lat", axis=2, tiled=True)
    pre_act = (
        jnp.einsum("ktd,kdc->ktc", inputs_full, enc_weight, preferred_element_type=jnp.float32)
        + enc_bias[:, None, :]
    )
    cut_level = 0.25 * thresholds.astype(jnp.float32)[:, None, :]
    gate_value = jax.nn.sigmoid((pre_act - cut_level) / jump_width)
    latent_act = (pre_act * gate_value).astype(jnp.bfloat16)
    rebuilt_first = jnp.dot(latent_act[0], same_dec[0], preferred_element_type=jnp.float32)
    rebuilt_second = jnp.dot(
        latent_act[1], same_dec[1], preferred_element_type=jnp.float32
    ) + jnp.dot(latent_act[0], next_dec[0], preferred_element_type=jnp.float32)
    far_weight = shifted(cross_dec, "sec", -1)
    source_act = jnp.where(leading, latent_act, jnp.zeros_like(latent_act))
    near_part = jnp.einsum(
        "ktc,kcd->td", source_act, cross_dec[0], preferred_element_type=jnp.float32
    )
    far_part = jnp.einsum(
        "ktc,kcd->td", source_act, far_weight[0], preferred_element_type=jnp.float32
    )
    partials = jnp.stack([rebuilt_first, rebuilt_second, near_part, far_part])
    summed = lax.psum_scatter(partials, "lat", scatter_dimension=2, tiled=True)
    crossing = shifted(summed[2:], "sec", 1)
    rebuilt = summed[:2] + crossing
    misfit = rebuilt - mlp_out.astype(jnp.float32)
    squared_total = lax.psum(jnp.sum(misfit * misfit), ("sec", "lat"))
    mean_square = squared_total / (4.0 * TOKENS * D)
    dy_rows = misfit.astype(jnp.bfloat16)
    extra_rows = shifted(dy_rows, "sec", -1)
    grad_full = lax.all_gather(
        jnp.concatenate([dy_rows, extra_rows], axis=0), "lat", axis=2, tiled=True
    )
    act_grad = jnp.stack(
        [
            back_dot(grad_full[0], same_dec[0]) + back_dot(grad_full[1], next_dec[0]),
            back_dot(grad_full[1], same_dec[1]),
        ]
    )
    cross_grad = jnp.einsum(
        "td,kcd->ktc", grad_full[2], cross_dec[0], preferred_element_type=jnp.float32
    )
    cross_grad = cross_grad + jnp.einsum(
        "td,kcd->ktc", grad_full[3], far_weight[0], preferred_element_type=jnp.float32
    )
    act_grad = act_grad + cross_grad
    gate_slope = gate_value + pre_act * gate_value * (1.0 - gate_value) / jump_width
    pre_grad = act_grad * gate_slope
    grad_bias = jnp.sum(pre_grad, axis=1)
    pre_rounded = pre_grad.astype(jnp.bfloat16)
    grad_enc = jnp.einsum(
        "ktd,ktc->kdc", inputs_full, pre_rounded, preferred_element_type=jnp.float32
    ).astype(jnp.bfloat16)
    grad_same = jnp.stack(
        [outer_dot(latent_act[0], grad_full[0]), outer_dot(latent_act[1], grad_full[1])]
    ).astype(jnp.bfloat16)
    grad_next = outer_dot(latent_act[0], grad_full[1])[None].astype(jnp.bfloat16)
    near_grad = jnp.einsum(
        "ktc,td->kcd", source_act, grad_full[2], preferred_element_type=jnp.float32
    ).astype(jnp.bfloat16)
    far_grad = jnp.einsum(
        "ktc,td->kcd", source_act, grad_full[3], preferred_element_type=jnp.float32
    ).astype(jnp.bfloat16)
    far_back = shifted(far_grad, "sec", 1)
    grad_cross = jnp.where(leading, near_grad, far_back)[None]
    return (mean_square, grad_enc, grad_bias, grad_same, grad_next, grad_cross)


def solution(mesh):
    in_specs = (
        P("sec", None, "lat"),
        P("sec", None, "lat"),
        P("sec", None, "lat"),
        P("sec", "lat"),
        P("sec", "lat"),
        P("sec", "lat", None),
        P("sec", "lat", None),
        P("sec", None, "lat", None),
    )
    out_specs = (
        P(),
        P("sec", None, "lat"),
        P("sec", "lat"),
        P("sec", "lat", None),
        P("sec", "lat", None),
        P("sec", None, "lat", None),
    )
    return jax.shard_map(
        per_device, mesh=mesh, in_specs=in_specs, out_specs=out_specs, check_vma=False
    )
```

profile of v0, /device:TPU:0, one launch (start us, length us, event | category | flops | bytes accessed | tf_op | source)
XLA Modules:
  0.0 208.9 jit_solution(15887882356919361757)
XLA Ops:
  7.2 0.0 copy-start
  7.2 0.0 copy-start.4
  7.2 0.0 all-gather.3.cloned.1.call-start
  7.2 0.7 all-gather.3.cloned.1.call-update
  7.9 0.0 reduce-scatter.2.cloned.1.call-start
  8.0 1.3 collective-permute-start
  9.3 0.7 convert_multiply_fusion
  10.0 39.8 %all-gather.3.cloned.1.call-done = bf16[2,128,2048]{2,1,0:T(8,128)(2,1)} async-done(((bf16[2,128,128]{2,1,0:T(8,128)(2,1)}), bf16[2,128,2048]{2,1,0:T(8,128)(2,1)}) %all-gather.3.cloned.1.call-update) | async-done | bytes 1048592 | tf_op jit(solution)/shard_map/all_gather | solution.py:29
  49.7 0.0 copy-done
  49.7 1.7 fusion.30
  51.5 1.3 fusion.20
  52.7 0.0 copy-start.2
  52.8 0.3 convolution_bitcast_fusion.2
  53.1 0.3 fusion
  53.4 0.4 copy-done.2
  53.8 0.3 convolution_bitcast_fusion.1
  54.1 0.0 collective-permute-done
  54.1 0.3 convolution_bitcast_fusion
  54.5 2.2 %pad_maximum_fusion = f32[4,128,2048]{2,1,0:T(8,128)} fusion(f32[1,128,2048]{2,1,0:T(8,128)S(1)} %convolution_bitcast_fusion, f32[1,128,2048]{2,1,0:T(8,128)S(1)} %convolution_bitcast_fusion.1, f32[1,128,2048]{2,1,0:T(8,128)S(1)} %fusion, f32[1,128,2048]{2,1,0:T(8,128)S(1)} %convolution_bitcast_fusion.2), kind=kLoop, calls=%fused_computation | loop fusion | flops 3145728 | bytes 8388608 | tf_op jit(solution)/shard_map/stack | solution.py:49
  56.7 0.0 reduce-scatter.2.cloned.1.call-update
  56.7 0.0 all-gather.5.cloned.1.call-start
  56.8 71.9 %reduce-scatter.2.cloned.1.call-done = f32[4,128,128]{2,1,0:T(8,128)} async-done(((f32[4,128,2048]{2,1,0:T(8,128)}), f32[4,128,128]{2,1,0:T(8,128)}) %reduce-scatter.2.cloned.1.call-update) | async-done | bytes 262160 | tf_op jit(solution)/shard_map/reduce_scatter | solution.py:50
  128.7 0.9 slice.55
  129.6 3.4 %collective-permute-start.1 = (f32[2,128,128]{2,1,0:T(8,128)S(1)}, f32[2,128,128]{2,1,0:T(8,128)S(1)}, u32[]{:S(2)}, u32[]{:S(2)}) collective-permute-start(f32[2,128,128]{2,1,0:T(8,128)S(1)} %slice.55), channel_id=1, source_target_pairs={{0,16},{1,17},{2,18},{3,19},{4,20},{5,21},{6,22},{7,23},{8,24},{9,... | collective-permute-start | bytes 393224 | tf_op jit(solution)/shard_map/ppermute | solution.py:14
  133.0 2.5 %collective-permute-done.1 = f32[2,128,128]{2,1,0:T(8,128)S(1)} collective-permute-done((f32[2,128,128]{2,1,0:T(8,128)S(1)}, f32[2,128,128]{2,1,0:T(8,128)S(1)}, u32[]{:S(2)}, u32[]{:S(2)}) %collective-permute-start.1) | collective-permute-done | bytes 131104 | tf_op jit(solution)/shard_map/ppermute | solution.py:14
  135.5 0.0 copy-done.6
  135.5 1.6 fusion.36
  137.1 1.3 collective-permute-start.2
  138.4 4.9 %collective-permute-done.2 = bf16[2,128,128]{2,1,0:T(8,128)(2,1)S(1)} collective-permute-done((bf16[2,128,128]{2,1,0:T(8,128)(2,1)S(1)}, bf16[2,128,128]{2,1,0:T(8,128)(2,1)S(1)}, u32[]{:S(2)}, u32[]{:S(2)}) %collective-permute-start.2) | collective-permute-done | bytes 65568 | tf_op jit(solution)/shard_map/ppermute | solution.py:14
  143.2 0.7 pad_maximum_fusion.2
  143.9 0.0 all-gather.5.cloned.1.call-update
  143.9 39.2 %psum.7 = f32[]{:T(128)} all-reduce(f32[]{:T(128)} %get-tuple-element.7), channel_id=1, replica_groups=mesh['sec'=2,'lat'=16] {'sec','lat'}, use_global_device_ids=true, to_apply=%region_2.3 | all-reduce | flops 1 | bytes 8 | tf_op jit(solution)/shard_map/psum | solution.py:54
  183.7 0.5 all-gather.5.cloned.1.call-done
  184.3 1.5 convolution_convert_fusion
  185.7 3.7 %collective-permute-start.3 = (bf16[2,64,2048]{2,1,0:T(8,128)(2,1)S(1)}, bf16[2,64,2048]{2,1,0:T(8,128)(2,1)S(1)}, u32[]{:S(2)}, u32[]{:S(2)}) collective-permute-start(bf16[2,64,2048]{2,1,0:T(8,128)(2,1)S(1)} %convolution_convert_fusion), channel_id=1, source_target_pairs={{0,16},{1,17},{2,18},{3,19},{4,20},{5,21},{6,22},{7,23},{8,24},{9,... | collective-permute-start | bytes 1572872 | tf_op jit(solution)/shard_map/ppermute | solution.py:14
  189.5 1.3 fusion.5
  190.8 1.3 fusion.4
  192.0 0.8 pad_maximum_fusion.1
  192.9 0.3 convolution_bitcast_fusion.3
  193.2 0.3 fusion.16
  193.5 0.0 copy-start.3
  193.5 0.3 fusion.13
  193.8 0.3 fusion.10
  194.1 0.9 fusion.6
  195.0 1.0 fusion.41
  196.0 1.1 fusion.3
  197.1 3.0 %collective-permute-done.3 = bf16[2,64,2048]{2,1,0:T(8,128)(2,1)S(1)} collective-permute-done((bf16[2,64,2048]{2,1,0:T(8,128)(2,1)S(1)}, bf16[2,64,2048]{2,1,0:T(8,128)(2,1)S(1)}, u32[]{:S(2)}, u32[]{:S(2)}) %collective-permute-start.3) | collective-permute-done | bytes 524320 | tf_op jit(solution)/shard_map/ppermute | solution.py:14
  200.1 1.1 fusion.2
  (7 shorter events, 0.0 us)
Async XLA Ops:
  7.2 42.6 %copy-start = (bf16[2,2048,64]{1,2,0:T(8,128)(2,1)S(1)}, bf16[2,2048,64]{1,2,0:T(8,128)(2,1)}, u32[]{:S(2)}) copy-start(bf16[2,2048,64]{1,2,0:T(8,128)(2,1)} %param.10) | copy-start | bytes 1572868
  7.2 45.6 %copy-start.4 = (bf16[2,64,2048]{2,1,0:T(8,128)(2,1)S(1)}, bf16[2,64,2048]{2,1,0:T(8,128)(2,1)}, u32[]{:S(2)}) copy-start(bf16[2,64,2048]{2,1,0:T(8,128)(2,1)} %param.13) | copy-start | bytes 1572868
  7.2 42.5 %all-gather.3.cloned.1.call-start = ((), (), s32[]{:S(2)}) async-start(), calls=%async_computation.1 | async-start | bytes 1114112 | tf_op jit(solution)/shard_map/all_gather | solution.py:29
  7.9 120.8 %reduce-scatter.2.cloned.1.call-start = ((), (), s32[]{:S(2)}) async-start(), calls=%async_computation.2 | async-start | bytes 4456448 | tf_op jit(solution)/shard_map/reduce_scatter | solution.py:50
  8.0 46.1 %collective-permute-start = (bf16[1,2,64,2048]{3,2,1,0:T(8,128)(2,1)}, bf16[1,2,64,2048]{3,2,1,0:T(8,128)(2,1)S(1)}, u32[]{:S(2)}, u32[]{:S(2)}) collective-permute-start(bf16[1,2,64,2048]{3,2,1,0:T(8,128)(2,1)} %param.15), channel_id=1, source_target_pairs={{16,0},{17,1},{18,2},{19,3},{20,4},{21,5},{22,6},{23,7},{24,8},{25... | collective-permute-start | bytes 1572872 | tf_op jit(solution)/shard_map/ppermute | solution.py:14
  10.0 43.1 %copy-start.5 = (bf16[1,64,2048]{2,1,0:T(8,128)(2,1)S(1)}, bf16[1,64,2048]{2,1,0:T(8,128)(2,1)}, u32[]{:S(2)}) copy-start(bf16[1,64,2048]{2,1,0:T(8,128)(2,1)} %param.14) | copy-start | bytes 786436
  52.7 1.0 copy-start.2
  56.7 78.8 %copy-start.6 = (bf16[2,128,128]{2,1,0:T(8,128)(2,1)S(1)}, bf16[2,128,128]{2,1,0:T(8,128)(2,1)}, u32[]{:S(2)}) copy-start(bf16[2,128,128]{2,1,0:T(8,128)(2,1)} %param.9) | copy-start | bytes 196612
  56.7 127.5 %all-gather.5.cloned.1.call-start = ((), (), s32[]{:S(2)}) async-start(), calls=%async_computation.3 | async-start | bytes 2228224 | tf_op jit(solution)/shard_map/all_gather | solution.py:58
  129.6 5.9 %collective-permute-start.1 = (f32[2,128,128]{2,1,0:T(8,128)S(1)}, f32[2,128,128]{2,1,0:T(8,128)S(1)}, u32[]{:S(2)}, u32[]{:S(2)}) collective-permute-start(f32[2,128,128]{2,1,0:T(8,128)S(1)} %slice.55), channel_id=1, source_target_pairs={{0,16},{1,17},{2,18},{3,19},{4,20},{5,21},{6,22},{7,23},{8,24},{9,... | collective-permute-start | bytes 393224 | tf_op jit(solution)/shard_map/ppermute | solution.py:14
  137.1 6.1 %collective-permute-start.2 = (bf16[2,128,128]{2,1,0:T(8,128)(2,1)S(1)}, bf16[2,128,128]{2,1,0:T(8,128)(2,1)S(1)}, u32[]{:S(2)}, u32[]{:S(2)}) collective-permute-start(bf16[2,128,128]{2,1,0:T(8,128)(2,1)S(1)} %get-tuple-element.6), channel_id=1, source_target_pairs={{16,0},{17,1},{18,2},{19,3},{20,4},{21,5},{22,6},{23,7},{24,8},{25... | collective-permute-start | bytes 196616 | tf_op jit(solution)/shard_map/ppermute | solution.py:14
  184.3 8.6 %copy-start.1 = (bf16[4,128,2048]{2,1,0:T(8,128)(2,1)S(1)}, bf16[4,128,2048]{2,1,0:T(8,128)(2,1)}, u32[]{:S(2)}) copy-start(bf16[4,128,2048]{2,1,0:T(8,128)(2,1)} %all-gather.5.cloned.1.call-done) | copy-start | bytes 6291460
  185.7 14.4 %collective-permute-start.3 = (bf16[2,64,2048]{2,1,0:T(8,128)(2,1)S(1)}, bf16[2,64,2048]{2,1,0:T(8,128)(2,1)S(1)}, u32[]{:S(2)}, u32[]{:S(2)}) collective-permute-start(bf16[2,64,2048]{2,1,0:T(8,128)(2,1)S(1)} %convolution_convert_fusion), channel_id=1, source_target_pairs={{0,16},{1,17},{2,18},{3,19},{4,20},{5,21},{6,22},{7,23},{8,24},{9,... | collective-permute-start | bytes 1572872 | tf_op jit(solution)/shard_map/ppermute | solution.py:14
  193.5 2.5 %copy-start.3 = (bf16[2,128,2048]{2,1,0:T(8,128)(2,1)S(1)}, bf16[2,128,2048]{2,1,0:T(8,128)(2,1)}, u32[]{:S(2)}) copy-start(bf16[2,128,2048]{2,1,0:T(8,128)(2,1)} %all-gather.3.cloned.1.call-done) | copy-start | bytes 3145732
Sparse Core Ops, SparseCore 0:
  10.2 39.4 all-gather.2
  56.8 71.8 reduce-scatter.1
  144.0 40.1 all-gather.4
where the time goes:
time: 209 us
  waiting for transfers between devices  123 us (59%)
  blocking collectives  39.2 us (19%)
  between operations  15.7 us (8%)
  matrix products  13.5 us (6%)
  starting transfers between devices  9.81 us (5%)
  other arithmetic  5.98 us (3%)
    reduce_scatter x1, waiting for transfers between devices, per_device(): summed = lax.psum_scatter(partials, 'lat', scatter_dimension=2, tiled=True)  71.9 us
    all_gather x1, waiting for transfers between devices, per_device(): inputs_full = lax.all_gather(resid_in, 'lat', axis=2, tiled=True)  39.8 us
    psum x1, blocking collectives, per_device(): squared_total = lax.psum(jnp.sum(misfit * misfit), ('sec', 'lat'))  39.2 us
    ppermute x4, waiting for transfers between devices, shifted(): lax.ppermute(value, axis, [(source, source + steps) for source in range(f...  10.4 us
    ppermute x4, starting transfers between devices, shifted(): lax.ppermute(value, axis, [(source, source + steps) for source in range(f...  9.69 us
  transfers between devices with their start and end apart: 7, of which 6 were waited for; matrix products, arithmetic and copies ran while one was open for 6% of the time, Pallas kernels for 0%

commit v1 on v0

--- a/solution.py
+++ b/solution.py
@@ -26,7 +26,12 @@
 
 def per_device(resid_in, mlp_out, enc_weight, enc_bias, thresholds, same_dec, next_dec, cross_dec):
     leading = lax.axis_index("sec") == 0
-    inputs_full = lax.all_gather(resid_in, "lat", axis=2, tiled=True)
+    ring = [resid_in]
+    for hop in range(15):
+        ring.append(lax.ppermute(ring[-1], "lat", [(dev, (dev + 1) % 16) for dev in range(16)]))
+    inputs_full = jnp.roll(
+        jnp.concatenate(ring[::-1], axis=2), (lax.axis_index("lat") + 1) * ring[0].shape[2], axis=2
+    )
     pre_act = (
         jnp.einsum("ktd,kdc->ktc", inputs_full, enc_weight, preferred_element_type=jnp.float32)
         + enc_bias[:, None, :]

time: 209 us -> 268 us (1.28)
  waiting for transfers between devices: 123 us -> 175 us
  local copies, waits for them, and re-layouts: 1.32 us -> 6.22 us
    ppermute x0 -> x15, waiting for transfers between devices: none -> 95 us  [per_device(): lax.ppermute(ring[-1], 'lat', [(dev, (dev + 1) % 16) for dev in range(16)])]
    all_gather x1 -> x0, waiting for transfers between devices: 39.8 us -> none  [per_device(): inputs_full = lax.all_gather(resid_in, 'lat', axis=2, tiled=True)]
    unnamed x14 -> x51, local copies, waits for them, and re-layouts: 0.41 us -> 5.28 us
  transfers between devices with their start and end apart: 7 -> 21, of which waited for: 6 -> 20; matrix products, arithmetic and copies ran while one was open for 6% -> 6% of each run, Pallas kernels for 0% -> 0%
where the time goes in v1:
time: 268 us; the launch traced here: 267 us
  waiting for transfers between devices  175 us (65%)
  blocking collectives  39.2 us (15%)
  between operations  16.2 us (6%)
  matrix products  14.1 us (5%)
  starting transfers between devices  10.2 us (4%)
  local copies, waits for them, and re-layouts  6.22 us (2%)
  other arithmetic  5.96 us (2%)
    ppermute x15, waiting for transfers between devices, per_device(): lax.ppermute(ring[-1], 'lat', [(dev, (dev + 1) % 16) for dev in range(16)])  95 us
    reduce_scatter x1, waiting for transfers between devices, per_device(): summed = lax.psum_scatter(partials, 'lat', scatter_dimension=2, tiled=True)  70.5 us
    psum x1, blocking collectives, per_device(): squared_total = lax.psum(jnp.sum(misfit * misfit), ('sec', 'lat'))  39.2 us
    ppermute x4, starting transfers between devices, shifted(): lax.ppermute(value, axis, [(source, source + steps) for source in range(f...  9.58 us
    ppermute x4, waiting for transfers between devices, shifted(): lax.ppermute(value, axis, [(source, source + steps) for source in range(f...  9.33 us
  transfers between devices with their start and end apart: 21, of which 20 were waited for; matrix products, arithmetic and copies ran while one was open for 6% of the time, Pallas kernels for 0%

profile of v1, /device:TPU:0, one launch (start us, length us, event | category | flops | bytes accessed | tf_op | source)
XLA Modules:
  0.0 267.2 jit_solution(1229855023415377547)
XLA Ops:
  7.2 0.5 collective-permute-start
  7.7 7.2 %collective-permute-done = bf16[2,128,128]{2,1,0:T(8,128)(2,1)S(1)} collective-permute-done((bf16[2,128,128]{2,1,0:T(8,128)(2,1)}, bf16[2,128,128]{2,1,0:T(8,128)(2,1)S(1)}, u32[]{:S(2)}, u32[]{:S(2)}) %collective-permute-start) | collective-permute-done | bytes 65568 | tf_op jit(solution)/shard_map/ppermute | solution.py:31
  14.9 6.4 %collective-permute-done.1 = bf16[2,128,128]{2,1,0:T(8,128)(2,1)S(1)} collective-permute-done((bf16[2,128,128]{2,1,0:T(8,128)(2,1)S(1)}, bf16[2,128,128]{2,1,0:T(8,128)(2,1)S(1)}, u32[]{:S(2)}, u32[]{:S(2)}) %collective-permute-start.1) | collective-permute-done | bytes 65568 | tf_op jit(solution)/shard_map/ppermute | solution.py:31
  21.3 6.4 %collective-permute-done.2 = bf16[2,128,128]{2,1,0:T(8,128)(2,1)S(1)} collective-permute-done((bf16[2,128,128]{2,1,0:T(8,128)(2,1)S(1)}, bf16[2,128,128]{2,1,0:T(8,128)(2,1)S(1)}, u32[]{:S(2)}, u32[]{:S(2)}) %collective-permute-start.2) | collective-permute-done | bytes 65568 | tf_op jit(solution)/shard_map/ppermute | solution.py:31
  27.7 6.4 %collective-permute-done.3 = bf16[2,128,128]{2,1,0:T(8,128)(2,1)S(1)} collective-permute-done((bf16[2,128,128]{2,1,0:T(8,128)(2,1)S(1)}, bf16[2,128,128]{2,1,0:T(8,128)(2,1)S(1)}, u32[]{:S(2)}, u32[]{:S(2)}) %collective-permute-start.3) | collective-permute-done | bytes 65568 | tf_op jit(solution)/shard_map/ppermute | solution.py:31
  34.1 6.4 %collective-permute-done.4 = bf16[2,128,128]{2,1,0:T(8,128)(2,1)S(1)} collective-permute-done((bf16[2,128,128]{2,1,0:T(8,128)(2,1)S(1)}, bf16[2,128,128]{2,1,0:T(8,128)(2,1)S(1)}, u32[]{:S(2)}, u32[]{:S(2)}) %collective-permute-start.4) | collective-permute-done | bytes 65568 | tf_op jit(solution)/shard_map/ppermute | solution.py:31
  40.5 6.4 %collective-permute-done.5 = bf16[2,128,128]{2,1,0:T(8,128)(2,1)S(1)} collective-permute-done((bf16[2,128,128]{2,1,0:T(8,128)(2,1)S(1)}, bf16[2,128,128]{2,1,0:T(8,128)(2,1)S(1)}, u32[]{:S(2)}, u32[]{:S(2)}) %collective-permute-start.5) | collective-permute-done | bytes 65568 | tf_op jit(solution)/shard_map/ppermute | solution.py:31
  46.8 6.4 %collective-permute-done.6 = bf16[2,128,128]{2,1,0:T(8,128)(2,1)S(1)} collective-permute-done((bf16[2,128,128]{2,1,0:T(8,128)(2,1)S(1)}, bf16[2,128,128]{2,1,0:T(8,128)(2,1)S(1)}, u32[]{:S(2)}, u32[]{:S(2)}) %collective-permute-start.6) | collective-permute-done | bytes 65568 | tf_op jit(solution)/shard_map/ppermute | solution.py:31
  53.2 6.4 %collective-permute-done.7 = bf16[2,128,128]{2,1,0:T(8,128)(2,1)S(1)} collective-permute-done((bf16[2,128,128]{2,1,0:T(8,128)(2,1)S(1)}, bf16[2,128,128]{2,1,0:T(8,128)(2,1)S(1)}, u32[]{:S(2)}, u32[]{:S(2)}) %collective-permute-start.7) | collective-permute-done | bytes 65568 | tf_op jit(solution)/shard_map/ppermute | solution.py:31
  59.6 6.4 %collective-permute-done.8 = bf16[2,128,128]{2,1,0:T(8,128)(2,1)S(1)} collective-permute-done((bf16[2,128,128]{2,1,0:T(8,128)(2,1)S(1)}, bf16[2,128,128]{2,1,0:T(8,128)(2,1)S(1)}, u32[]{:S(2)}, u32[]{:S(2)}) %collective-permute-start.8) | collective-permute-done | bytes 65568 | tf_op jit(solution)/shard_map/ppermute | solution.py:31
  66.0 6.4 %collective-permute-done.9 = bf16[2,128,128]{2,1,0:T(8,128)(2,1)S(1)} collective-permute-done((bf16[2,128,128]{2,1,0:T(8,128)(2,1)S(1)}, bf16[2,128,128]{2,1,0:T(8,128)(2,1)S(1)}, u32[]{:S(2)}, u32[]{:S(2)}) %collective-permute-start.9) | collective-permute-done | bytes 65568 | tf_op jit(solution)/shard_map/ppermute | solution.py:31
  72.4 6.4 %collective-permute-done.10 = bf16[2,128,128]{2,1,0:T(8,128)(2,1)S(1)} collective-permute-done((bf16[2,128,128]{2,1,0:T(8,128)(2,1)S(1)}, bf16[2,128,128]{2,1,0:T(8,128)(2,1)S(1)}, u32[]{:S(2)}, u32[]{:S(2)}) %collective-permute-start.10) | collective-permute-done | bytes 65568 | tf_op jit(solution)/shard_map/ppermute | solution.py:31
  78.8 6.4 %collective-permute-done.11 = bf16[2,128,128]{2,1,0:T(8,128)(2,1)S(1)} collective-permute-done((bf16[2,128,128]{2,1,0:T(8,128)(2,1)S(1)}, bf16[2,128,128]{2,1,0:T(8,128)(2,1)S(1)}, u32[]{:S(2)}, u32[]{:S(2)}) %collective-permute-start.11) | collective-permute-done | bytes 65568 | tf_op jit(solution)/shard_map/ppermute | solution.py:31
  85.2 6.4 %collective-permute-done.12 = bf16[2,128,128]{2,1,0:T(8,128)(2,1)S(1)} collective-permute-done((bf16[2,128,128]{2,1,0:T(8,128)(2,1)S(1)}, bf16[2,128,128]{2,1,0:T(8,128)(2,1)S(1)}, u32[]{:S(2)}, u32[]{:S(2)}) %collective-permute-start.12) | collective-permute-done | bytes 65568 | tf_op jit(solution)/shard_map/ppermute | solution.py:31
  91.6 1.3 collective-permute-start.15
  92.9 5.2 %collective-permute-done.13 = bf16[2,128,128]{2,1,0:T(8,128)(2,1)} collective-permute-done((bf16[2,128,128]{2,1,0:T(8,128)(2,1)S(1)}, bf16[2,128,128]{2,1,0:T(8,128)(2,1)}, u32[]{:S(2)}, u32[]{:S(2)}) %collective-permute-start.13) | collective-permute-done | bytes 65568 | tf_op jit(solution)/shard_map/ppermute | solution.py:31
  98.1 0.7 convert_multiply_fusion
  98.7 6.0 %collective-permute-done.14 = bf16[2,128,128]{2,1,0:T(8,128)(2,1)} collective-permute-done((bf16[2,128,128]{2,1,0:T(8,128)(2,1)}, bf16[2,128,128]{2,1,0:T(8,128)(2,1)}, u32[]{:S(2)}, u32[]{:S(2)}) %collective-permute-start.14) | collective-permute-done | bytes 65568 | tf_op jit(solution)/shard_map/ppermute | solution.py:31
  104.8 0.9 constant_dynamic-update-slice_fusion.31
  105.6 0.9 constant_dynamic-update-slice_fusion.30
  106.8 0.9 constant_dynamic-update-slice_fusion.16
  107.7 0.9 constant_dynamic-update-slice_fusion.15
  108.6 0.9 constant_dynamic-update-slice_fusion.14
  109.9 1.1 fusion.31
  112.0 0.4 copy-done.2
  112.4 0.3 convolution_bitcast_fusion.1
  112.7 1.4 convolution_bitcast_fusion
  114.1 2.2 pad_maximum_fusion
  116.3 70.5 %reduce-scatter.2.cloned.1.call-done = f32[4,128,128]{2,1,0:T(8,128)} async-done(((f32[4,128,2048]{2,1,0:T(8,128)}), f32[4,128,128]{2,1,0:T(8,128)}) %reduce-scatter.2.cloned.1.call-update) | async-done | bytes 262160 | tf_op jit(solution)/shard_map/reduce_scatter | solution.py:55
  186.9 0.9 slice.55
  187.8 3.3 %collective-permute-start.16 = (f32[2,128,128]{2,1,0:T(8,128)S(1)}, f32[2,128,128]{2,1,0:T(8,128)S(1)}, u32[]{:S(2)}, u32[]{:S(2)}) collective-permute-start(f32[2,128,128]{2,1,0:T(8,128)S(1)} %slice.55), channel_id=1, source_target_pairs={{0,16},{1,17},{2,18},{3,19},{4,20},{5,21},{6,22},{7,23},{8,24},{9,... | collective-permute-start | bytes 393224 | tf_op jit(solution)/shard_map/ppermute | solution.py:14
  191.1 2.5 collective-permute-done.16
  193.6 1.6 fusion.37
  195.1 1.3 collective-permute-start.17
  196.4 4.9 %collective-permute-done.17 = bf16[2,128,128]{2,1,0:T(8,128)(2,1)S(1)} collective-permute-done((bf16[2,128,128]{2,1,0:T(8,128)(2,1)S(1)}, bf16[2,128,128]{2,1,0:T(8,128)(2,1)S(1)}, u32[]{:S(2)}, u32[]{:S(2)}) %collective-permute-start.17) | collective-permute-done | bytes 65568 | tf_op jit(solution)/shard_map/ppermute | solution.py:14
  201.3 0.7 pad_maximum_fusion.2
  201.9 39.2 %psum.7 = f32[]{:T(128)} all-reduce(f32[]{:T(128)} %get-tuple-element.7), channel_id=1, replica_groups=mesh['sec'=2,'lat'=16] {'sec','lat'}, use_global_device_ids=true, to_apply=%region_2.3 | all-reduce | flops 1 | bytes 8 | tf_op jit(solution)/shard_map/psum | solution.py:59
  241.8 0.5 all-gather.2.cloned.1.call-done
  242.3 1.5 convolution_convert_fusion.1
  243.8 3.7 %collective-permute-start.18 = (bf16[2,64,2048]{2,1,0:T(8,128)(2,1)S(1)}, bf16[2,64,2048]{2,1,0:T(8,128)(2,1)S(1)}, u32[]{:S(2)}, u32[]{:S(2)}) collective-permute-start(bf16[2,64,2048]{2,1,0:T(8,128)(2,1)S(1)} %convolution_convert_fusion.1), channel_id=1, source_target_pairs={{0,16},{1,17},{2,18},{3,19},{4,20},{5,21},{6,22},{7,23},{8,24},{9,... | collective-permute-start | bytes 1572872 | tf_op jit(solution)/shard_map/ppermute | solution.py:14
  247.6 1.3 fusion.4
  248.8 1.3 fusion.3
  250.1 0.8 pad_maximum_fusion.1
  252.2 0.9 fusion.5
  253.1 2.0 fusion.44
  255.1 1.1 convolution_convert_fusion
  256.2 2.0 collective-permute-done.18
  258.2 1.1 fusion.2
  (72 shorter events, 2.9 us)
Async XLA Ops:
  7.2 102.7 %copy-start = (bf16[2,2048,64]{1,2,0:T(8,128)(2,1)S(1)}, bf16[2,2048,64]{1,2,0:T(8,128)(2,1)}, u32[]{:S(2)}) copy-start(bf16[2,2048,64]{1,2,0:T(8,128)(2,1)} %param.10) | copy-start | bytes 1572868
  7.2 102.6 %copy-start.6 = (bf16[2,128,128]{2,1,0:T(8,128)(2,1)S(1)}, bf16[2,128,128]{2,1,0:T(8,128)(2,1)}, u32[]{:S(2)}) copy-start(bf16[2,128,128]{2,1,0:T(8,128)(2,1)} %param.8) | copy-start | bytes 196612
  7.2 179.7 %reduce-scatter.2.cloned.1.call-start = ((), (), s32[]{:S(2)}) async-start(), calls=%async_computation.1 | async-start | bytes 4456448 | tf_op jit(solution)/shard_map/reduce_scatter | solution.py:55
  7.2 7.7 %collective-permute-start = (bf16[2,128,128]{2,1,0:T(8,128)(2,1)}, bf16[2,128,128]{2,1,0:T(8,128)(2,1)S(1)}, u32[]{:S(2)}, u32[]{:S(2)}) collective-permute-start(bf16[2,128,128]{2,1,0:T(8,128)(2,1)} %param.8), channel_id=1, source_target_pairs={{0,1},{1,2},{2,3},{3,4},{4,5},{5,6},{6,7},{7,8},{8,9},{9,10},{10,1... | collective-permute-start | bytes 196616 | tf_op jit(solution)/shard_map/ppermute | solution.py:31
  14.9 6.4 %collective-permute-start.1 = (bf16[2,128,128]{2,1,0:T(8,128)(2,1)S(1)}, bf16[2,128,128]{2,1,0:T(8,128)(2,1)S(1)}, u32[]{:S(2)}, u32[]{:S(2)}) collective-permute-start(bf16[2,128,128]{2,1,0:T(8,128)(2,1)S(1)} %collective-permute-done), channel_id=1, source_target_pairs={{0,1},{1,2},{2,3},{3,4},{4,5},{5,6},{6,7},{7,8},{8,9},{9,10},{10,1... | collective-permute-start | bytes 196616 | tf_op jit(solution)/shard_map/ppermute | solution.py:31
  21.3 6.4 %collective-permute-start.2 = (bf16[2,128,128]{2,1,0:T(8,128)(2,1)S(1)}, bf16[2,128,128]{2,1,0:T(8,128)(2,1)S(1)}, u32[]{:S(2)}, u32[]{:S(2)}) collective-permute-start(bf16[2,128,128]{2,1,0:T(8,128)(2,1)S(1)} %collective-permute-done.1), channel_id=1, source_target_pairs={{0,1},{1,2},{2,3},{3,4},{4,5},{5,6},{6,7},{7,8},{8,9},{9,10},{10,1... | collective-permute-start | bytes 196616 | tf_op jit(solution)/shard_map/ppermute | solution.py:31
  27.7 6.4 %collective-permute-start.3 = (bf16[2,128,128]{2,1,0:T(8,128)(2,1)S(1)}, bf16[2,128,128]{2,1,0:T(8,128)(2,1)S(1)}, u32[]{:S(2)}, u32[]{:S(2)}) collective-permute-start(bf16[2,128,128]{2,1,0:T(8,128)(2,1)S(1)} %collective-permute-done.2), channel_id=1, source_target_pairs={{0,1},{1,2},{2,3},{3,4},{4,5},{5,6},{6,7},{7,8},{8,9},{9,10},{10,1... | collective-permute-start | bytes 196616 | tf_op jit(solution)/shard_map/ppermute | solution.py:31
  34.1 6.4 %collective-permute-start.4 = (bf16[2,128,128]{2,1,0:T(8,128)(2,1)S(1)}, bf16[2,128,128]{2,1,0:T(8,128)(2,1)S(1)}, u32[]{:S(2)}, u32[]{:S(2)}) collective-permute-start(bf16[2,128,128]{2,1,0:T(8,128)(2,1)S(1)} %collective-permute-done.3), channel_id=1, source_target_pairs={{0,1},{1,2},{2,3},{3,4},{4,5},{5,6},{6,7},{7,8},{8,9},{9,10},{10,1... | collective-permute-start | bytes 196616 | tf_op jit(solution)/shard_map/ppermute | solution.py:31
  40.5 6.4 %collective-permute-start.5 = (bf16[2,128,128]{2,1,0:T(8,128)(2,1)S(1)}, bf16[2,128,128]{2,1,0:T(8,128)(2,1)S(1)}, u32[]{:S(2)}, u32[]{:S(2)}) collective-permute-start(bf16[2,128,128]{2,1,0:T(8,128)(2,1)S(1)} %collective-permute-done.4), channel_id=1, source_target_pairs={{0,1},{1,2},{2,3},{3,4},{4,5},{5,6},{6,7},{7,8},{8,9},{9,10},{10,1... | collective-permute-start | bytes 196616 | tf_op jit(solution)/shard_map/ppermute | solution.py:31
  46.8 6.4 %collective-permute-start.6 = (bf16[2,128,128]{2,1,0:T(8,128)(2,1)S(1)}, bf16[2,128,128]{2,1,0:T(8,128)(2,1)S(1)}, u32[]{:S(2)}, u32[]{:S(2)}) collective-permute-start(bf16[2,128,128]{2,1,0:T(8,128)(2,1)S(1)} %collective-permute-done.5), channel_id=1, source_target_pairs={{0,1},{1,2},{2,3},{3,4},{4,5},{5,6},{6,7},{7,8},{8,9},{9,10},{10,1... | collective-permute-start | bytes 196616 | tf_op jit(solution)/shard_map/ppermute | solution.py:31
  53.2 6.4 %collective-permute-start.7 = (bf16[2,128,128]{2,1,0:T(8,128)(2,1)S(1)}, bf16[2,128,128]{2,1,0:T(8,128)(2,1)S(1)}, u32[]{:S(2)}, u32[]{:S(2)}) collective-permute-start(bf16[2,128,128]{2,1,0:T(8,128)(2,1)S(1)} %collective-permute-done.6), channel_id=1, source_target_pairs={{0,1},{1,2},{2,3},{3,4},{4,5},{5,6},{6,7},{7,8},{8,9},{9,10},{10,1... | collective-permute-start | bytes 196616 | tf_op jit(solution)/shard_map/ppermute | solution.py:31
  59.6 6.4 %collective-permute-start.8 = (bf16[2,128,128]{2,1,0:T(8,128)(2,1)S(1)}, bf16[2,128,128]{2,1,0:T(8,128)(2,1)S(1)}, u32[]{:S(2)}, u32[]{:S(2)}) collective-permute-start(bf16[2,128,128]{2,1,0:T(8,128)(2,1)S(1)} %collective-permute-done.7), channel_id=1, source_target_pairs={{0,1},{1,2},{2,3},{3,4},{4,5},{5,6},{6,7},{7,8},{8,9},{9,10},{10,1... | collective-permute-start | bytes 196616 | tf_op jit(solution)/shard_map/ppermute | solution.py:31
  66.0 6.4 %collective-permute-start.9 = (bf16[2,128,128]{2,1,0:T(8,128)(2,1)S(1)}, bf16[2,128,128]{2,1,0:T(8,128)(2,1)S(1)}, u32[]{:S(2)}, u32[]{:S(2)}) collective-permute-start(bf16[2,128,128]{2,1,0:T(8,128)(2,1)S(1)} %collective-permute-done.8), channel_id=1, source_target_pairs={{0,1},{1,2},{2,3},{3,4},{4,5},{5,6},{6,7},{7,8},{8,9},{9,10},{10,1... | collective-permute-start | bytes 196616 | tf_op jit(solution)/shard_map/ppermute | solution.py:31
  72.4 6.4 %collective-permute-start.10 = (bf16[2,128,128]{2,1,0:T(8,128)(2,1)S(1)}, bf16[2,128,128]{2,1,0:T(8,128)(2,1)S(1)}, u32[]{:S(2)}, u32[]{:S(2)}) collective-permute-start(bf16[2,128,128]{2,1,0:T(8,128)(2,1)S(1)} %collective-permute-done.9), channel_id=1, source_target_pairs={{0,1},{1,2},{2,3},{3,4},{4,5},{5,6},{6,7},{7,8},{8,9},{9,10},{10,1... | collective-permute-start | bytes 196616 | tf_op jit(solution)/shard_map/ppermute | solution.py:31
  78.8 6.4 %collective-permute-start.11 = (bf16[2,128,128]{2,1,0:T(8,128)(2,1)S(1)}, bf16[2,128,128]{2,1,0:T(8,128)(2,1)S(1)}, u32[]{:S(2)}, u32[]{:S(2)}) collective-permute-start(bf16[2,128,128]{2,1,0:T(8,128)(2,1)S(1)} %collective-permute-done.10), channel_id=1, source_target_pairs={{0,1},{1,2},{2,3},{3,4},{4,5},{5,6},{6,7},{7,8},{8,9},{9,10},{10,1... | collective-permute-start | bytes 196616 | tf_op jit(solution)/shard_map/ppermute | solution.py:31
  85.2 6.4 %collective-permute-start.12 = (bf16[2,128,128]{2,1,0:T(8,128)(2,1)S(1)}, bf16[2,128,128]{2,1,0:T(8,128)(2,1)S(1)}, u32[]{:S(2)}, u32[]{:S(2)}) collective-permute-start(bf16[2,128,128]{2,1,0:T(8,128)(2,1)S(1)} %collective-permute-done.11), channel_id=1, source_target_pairs={{0,1},{1,2},{2,3},{3,4},{4,5},{5,6},{6,7},{7,8},{8,9},{9,10},{10,1... | collective-permute-start | bytes 196616 | tf_op jit(solution)/shard_map/ppermute | solution.py:31
  91.6 6.5 %collective-permute-start.13 = (bf16[2,128,128]{2,1,0:T(8,128)(2,1)S(1)}, bf16[2,128,128]{2,1,0:T(8,128)(2,1)}, u32[]{:S(2)}, u32[]{:S(2)}) collective-permute-start(bf16[2,128,128]{2,1,0:T(8,128)(2,1)S(1)} %collective-permute-done.12), channel_id=1, source_target_pairs={{0,1},{1,2},{2,3},{3,4},{4,5},{5,6},{6,7},{7,8},{8,9},{9,10},{10,1... | collective-permute-start | bytes 196616 | tf_op jit(solution)/shard_map/ppermute | solution.py:31
  91.6 21.1 %collective-permute-start.15 = (bf16[1,2,64,2048]{3,2,1,0:T(8,128)(2,1)}, bf16[1,2,64,2048]{3,2,1,0:T(8,128)(2,1)}, u32[]{:S(2)}, u32[]{:S(2)}) collective-permute-start(bf16[1,2,64,2048]{3,2,1,0:T(8,128)(2,1)} %param.15), channel_id=1, source_target_pairs={{16,0},{17,1},{18,2},{19,3},{20,4},{21,5},{22,6},{23,7},{24,8},{25... | collective-permute-start | bytes 1572872 | tf_op jit(solution)/shard_map/ppermute | solution.py:14
  98.1 6.7 %collective-permute-start.14 = (bf16[2,128,128]{2,1,0:T(8,128)(2,1)}, bf16[2,128,128]{2,1,0:T(8,128)(2,1)}, u32[]{:S(2)}, u32[]{:S(2)}) collective-permute-start(bf16[2,128,128]{2,1,0:T(8,128)(2,1)} %collective-permute-done.13), channel_id=1, source_target_pairs={{0,1},{1,2},{2,3},{3,4},{4,5},{5,6},{6,7},{7,8},{8,9},{9,10},{10,1... | collective-permute-start | bytes 196616 | tf_op jit(solution)/shard_map/ppermute | solution.py:31
  98.7 11.1 %copy-start.8 = (f32[2,64]{1,0:T(2,128)S(1)}, f32[2,64]{1,0:T(2,128)}, u32[]{:S(2)}) copy-start(f32[2,64]{1,0:T(2,128)} %param.11) | copy-start | bytes 1540
  106.8 4.2 %copy-start.3 = (bf16[2,64,2048]{2,1,0:T(8,128)(2,1)S(1)}, bf16[2,64,2048]{2,1,0:T(8,128)(2,1)}, u32[]{:S(2)}) copy-start(bf16[2,64,2048]{2,1,0:T(8,128)(2,1)} %param.13) | copy-start | bytes 1572868
  109.9 1.8 copy-start.5
  111.3 1.0 copy-start.2
  116.3 77.3 %copy-start.7 = (bf16[2,128,128]{2,1,0:T(8,128)(2,1)S(1)}, bf16[2,128,128]{2,1,0:T(8,128)(2,1)}, u32[]{:S(2)}) copy-start(bf16[2,128,128]{2,1,0:T(8,128)(2,1)} %param.9) | copy-start | bytes 196612
  116.3 126.0 %all-gather.2.cloned.1.call-start = ((), (), s32[]{:S(2)}) async-start(), calls=%async_computation.2 | async-start | bytes 2228224 | tf_op jit(solution)/shard_map/all_gather | solution.py:63
  187.8 5.8 %collective-permute-start.16 = (f32[2,128,128]{2,1,0:T(8,128)S(1)}, f32[2,128,128]{2,1,0:T(8,128)S(1)}, u32[]{:S(2)}, u32[]{:S(2)}) collective-permute-start(f32[2,128,128]{2,1,0:T(8,128)S(1)} %slice.55), channel_id=1, source_target_pairs={{0,16},{1,17},{2,18},{3,19},{4,20},{5,21},{6,22},{7,23},{8,24},{9,... | collective-permute-start | bytes 393224 | tf_op jit(solution)/shard_map/ppermute | solution.py:14
  195.1 6.1 %collective-permute-start.17 = (bf16[2,128,128]{2,1,0:T(8,128)(2,1)S(1)}, bf16[2,128,128]{2,1,0:T(8,128)(2,1)S(1)}, u32[]{:S(2)}, u32[]{:S(2)}) collective-permute-start(bf16[2,128,128]{2,1,0:T(8,128)(2,1)S(1)} %get-tuple-element.6), channel_id=1, source_target_pairs={{16,0},{17,1},{18,2},{19,3},{20,4},{21,5},{22,6},{23,7},{24,8},{25... | collective-permute-start | bytes 196616 | tf_op jit(solution)/shard_map/ppermute | solution.py:14
  242.3 8.6 %copy-start.1 = (bf16[4,128,2048]{2,1,0:T(8,128)(2,1)S(1)}, bf16[4,128,2048]{2,1,0:T(8,128)(2,1)}, u32[]{:S(2)}) copy-start(bf16[4,128,2048]{2,1,0:T(8,128)(2,1)} %all-gather.2.cloned.1.call-done) | copy-start | bytes 6291460
  242.3 8.6 %copy-start.4 = (bf16[2,64,2048]{2,1,0:T(8,128)(2,1)S(1)}, bf16[2,64,2048]{2,1,0:T(8,128)(2,1)}, u32[]{:S(2)}) copy-start(bf16[2,64,2048]{2,1,0:T(8,128)(2,1)} %param.13) | copy-start | bytes 1572868
  243.8 14.4 %collective-permute-start.18 = (bf16[2,64,2048]{2,1,0:T(8,128)(2,1)S(1)}, bf16[2,64,2048]{2,1,0:T(8,128)(2,1)S(1)}, u32[]{:S(2)}, u32[]{:S(2)}) collective-permute-start(bf16[2,64,2048]{2,1,0:T(8,128)(2,1)S(1)} %convolution_convert_fusion.1), channel_id=1, source_target_pairs={{0,16},{1,17},{2,18},{3,19},{4,20},{5,21},{6,22},{7,23},{8,24},{9,... | collective-permute-start | bytes 1572872 | tf_op jit(solution)/shard_map/ppermute | solution.py:14
  251.3 1.9 copy-start.9
Sparse Core Ops, SparseCore 0:
  116.4 70.3 reduce-scatter.1
  202.1 40.2 all-gather.1
